TPU v7x, 256 devices: a whole 4x4x8 slice. The times are simulated.
256 devices in a mesh: anim: 16 (over y, x_lo, core), snp: 16 (over z, x_hi).
Axes of the slice: x: 4 (x_hi: 2, x_lo: 2; x = x_hi * 2 + x_lo), y: 4, z: 8, core: 2. Of those that a mesh axis runs over, the one named last changes fastest.
Arguments:
- core_geno: bfloat16 [12288, 49152], P('anim', 'snp'), may hold values from -10 to 10, as said below
- noncore_geno: bfloat16 [12288, 49152], P('anim', 'snp'), may hold values from -10 to 10, as said below
- core_inv: bfloat16 [12288, 12288], P('anim', 'snp'), may hold values from -0.0546875 to 0.0546875
- snp_effects: bfloat16 [256, 49152], P(None, 'snp'), may hold values from -0.02734375 to 0.02734375
- noncore_scale: float32 [12288], P('anim'), may hold values from 0.5 to 2
Outputs:
- noncore_out: float32 [256, 12288], P(None, 'anim')
- core_out: float32 [256, 12288], P(None, ('anim', 'snp'))
Inputs may be any that keep to these rules, and one draw needn't show every extreme that they name: `core_geno`: each column j is (c - 2 p_j) / sqrt(2 p_j (1 - p_j)) for codes c in 0, 1, 2 and a column frequency p_j shared with noncore_geno. `noncore_geno`: each column j is (c - 2 p_j) / sqrt(2 p_j (1 - p_j)) for codes c in 0, 1, 2 and a column frequency p_j shared with core_geno.
All inputs are finite; a program needn't handle non-finite values.
Results may differ from a plain program's by a relative error of at most 0.008.
Values may be sent and summed in bfloat16 or wider, within the bound.
A program may use at most 64 MiB of HBM per device.

v0:
```python
import jax
import jax.numpy as jnp
from jax import lax
from jax.sharding import PartitionSpec as P

NSNP = 49152


def contract_last(left, right):
    return lax.dot_general(
        left, right, (((1,), (1,)), ((), ())), preferred_element_type=jnp.float32
    )


def core_columns(partial_value, base, tile_cols):
    snp_index = lax.axis_index("snp")
    summed = lax.psum(partial_value, "snp")
    value = summed if base is None else base.astype(jnp.float32) - summed
    block = value.astype(jnp.bfloat16)
    whole = lax.all_gather(block, "anim", axis=1, tiled=True)
    columns = lax.dynamic_slice_in_dim(whole, snp_index * tile_cols, tile_cols, 1)
    return (block, columns)


def marker_terms(partial_value):
    total = lax.psum(partial_value, "anim")
    return (total / NSNP).astype(jnp.bfloat16)


def local(core_geno, noncore_geno, core_inv, snp_effects, noncore_scale):
    tile_cols = core_inv.shape[1]
    core_partial = contract_last(snp_effects, core_geno)
    noncore_partial = contract_last(snp_effects, noncore_geno)
    core_vals, value_cols = core_columns(core_partial, None, tile_cols)
    noncore_vals = lax.psum(noncore_partial, "snp")
    weight_partial = contract_last(value_cols, core_inv)
    core_weights = lax.psum(weight_partial, "snp").astype(jnp.bfloat16)
    snp_core = marker_terms(jnp.dot(core_weights, core_geno, preferred_element_type=jnp.float32))
    predicted = lax.psum(contract_last(snp_core, noncore_geno), "snp")
    noncore_out = noncore_scale[None, :] * (noncore_vals - predicted)
    noncore_half = noncore_out.astype(jnp.bfloat16)
    snp_noncore = marker_terms(
        jnp.dot(noncore_half, noncore_geno, preferred_element_type=jnp.float32)
    )
    back_partial = contract_last(snp_noncore, core_geno)
    core_rest, rest_cols = core_columns(back_partial, core_vals, tile_cols)
    out_partial = contract_last(rest_cols, core_inv)
    core_out = lax.psum_scatter(out_partial, "snp", scatter_dimension=1, tiled=True)
    return (noncore_out, core_out)


def solution(mesh):
    return jax.shard_map(
        local,
        mesh=mesh,
        in_specs=(P("anim", "snp"), P("anim", "snp"), P("anim", "snp"), P(None, "snp"), P("anim")),
        out_specs=(P(None, "anim"), P(None, ("anim", "snp"))),
        check_vma=False,
    )
```

profile of v0, /device:TPU:8, one launch (start us, length us, event | category | flops | bytes accessed | tf_op | source)
XLA Modules:
  0.0 1105.2 jit_solution(17298598876535657185)
XLA Ops:
  7.2 0.0 copy-start
  7.2 0.0 copy-start.2
  7.2 0.0 all-gather.3.cloned.1.call-start
  7.2 1.3 copy-done
  8.6 3.8 fusion.17
  12.3 89.5 %all-reduce.15 = bf16[256,768]{1,0:T(8,128)(2,1)} all-reduce(f32[256,768]{1,0:T(8,128)S(1)} %fusion.17), channel_id=1, replica_groups=mesh['anim'=16,'snp'=16] {'snp'}, use_global_device_ids=true, to_apply=%region_1.0 | all-reduce | flops 196608 | bytes 1179648 | tf_op jit(solution)/shard_map/psum | solution.py:17
  101.8 0.0 all-gather.3.cloned.1.call-update
  101.9 0.0 all-reduce.8.cloned.1.call-start
  101.9 40.4 %all-gather.3.cloned.1.call-done = bf16[256,12288]{1,0:T(8,128)(2,1)} async-done(((bf16[256,768]{1,0:T(8,128)(2,1)}), bf16[256,12288]{1,0:T(8,128)(2,1)}) %all-gather.3.cloned.1.call-update) | async-done | bytes 6291472 | tf_op jit(solution)/shard_map/all_gather | solution.py:20
  142.3 0.0 copy-done.2
  142.3 1.5 fusion.10
  143.8 87.3 %all-reduce.16 = bf16[256,768]{1,0:T(8,128)(2,1)} all-reduce(f32[256,768]{1,0:T(8,128)S(1)} %fusion.10), channel_id=1, replica_groups=mesh['anim'=16,'snp'=16] {'snp'}, use_global_device_ids=true, to_apply=%region_2.0 | all-reduce | flops 196608 | bytes 1179648 | tf_op jit(solution)/shard_map/psum | solution.py:37
  231.1 5.5 fusion.18
  236.6 0.0 all-reduce.8.cloned.1.call-update
  236.6 0.0 all-reduce.14.cloned.1.call-start
  236.7 4.6 fusion.16
  241.3 0.0 copy-start.4
  241.3 121.1 %all-reduce.8.cloned.1.call-done = f32[256,3072]{1,0:T(8,128)} async-done(((f32[256,3072]{1,0:T(8,128)}), f32[256,3072]{1,0:T(8,128)}) %all-reduce.8.cloned.1.call-update) | async-done | bytes 3145744 | tf_op jit(solution)/shard_map/psum | solution.py:26
  362.4 5.6 fusion
  368.0 0.0 all-reduce.14.cloned.1.call-update
  368.0 0.0 all-reduce.10.cloned.1.call-start
  368.1 169.1 %all-reduce.14.cloned.1.call-done = (f32[256,768]{1,0:T(8,128)}, f32[256,768]{1,0:T(8,128)}) async-done(((f32[256,768]{1,0:T(8,128)}, f32[256,768]{1,0:T(8,128)}), (f32[256,768]{1,0:T(8,128)}, f32[256,768]{1,0:T(8,128)})) %all-reduce.14.cloned.1.call-update) | async-done | bytes 1572880 | tf_op jit(solution)/shard_map/psum | solution.py:35
  537.1 0.0 copy-done.4
  537.1 1.5 subtract_multiply_fusion
  538.6 0.0 copy-start.1
  538.6 5.7 fusion.6
  544.3 0.0 copy-done.1
  544.3 0.0 all-reduce.10.cloned.1.call-update
  544.3 0.0 copy-start.3
  544.4 0.0 all-reduce.12.cloned.1.call-start
  544.4 128.0 %all-reduce.10.cloned.1.call-done = f32[256,3072]{1,0:T(8,128)} async-done(((f32[256,3072]{1,0:T(8,128)}), f32[256,3072]{1,0:T(8,128)}) %all-reduce.10.cloned.1.call-update) | async-done | bytes 3145744 | tf_op jit(solution)/shard_map/psum | solution.py:26
  672.4 5.6 fusion.1
  678.0 0.0 all-reduce.12.cloned.1.call-update
  678.0 0.0 all-gather.5.cloned.1.call-start
  678.0 165.4 %all-reduce.12.cloned.1.call-done = f32[256,768]{1,0:T(8,128)} async-done(((f32[256,768]{1,0:T(8,128)}), f32[256,768]{1,0:T(8,128)}) %all-reduce.12.cloned.1.call-update) | async-done | bytes 786448 | tf_op jit(solution)/shard_map/psum | solution.py:17
  843.4 0.0 copy-done.3
  843.4 1.9 subtract_convert_fusion
  845.4 0.0 all-gather.5.cloned.1.call-update
  845.4 0.0 reduce-scatter.2.cloned.1.call-start
  845.4 42.9 %all-gather.5.cloned.1.call-done = bf16[256,12288]{1,0:T(8,128)(2,1)} async-done(((bf16[256,768]{1,0:T(8,128)(2,1)}), bf16[256,12288]{1,0:T(8,128)(2,1)}) %all-gather.5.cloned.1.call-update) | async-done | bytes 6291472 | tf_op jit(solution)/shard_map/all_gather | solution.py:20
  888.4 2.4 fusion.4
  890.7 0.0 reduce-scatter.2.cloned.1.call-update
  890.8 207.5 %reduce-scatter.2.cloned.1.call-done = f32[256,48]{0,1:T(8,128)} async-done(((f32[256,768]{0,1:T(8,128)}), f32[256,48]{0,1:T(8,128)}) %reduce-scatter.2.cloned.1.call-update) | async-done | bytes 49168 | tf_op jit(solution)/shard_map/reduce_scatter | solution.py:48
Async XLA Ops:
  7.2 1.4 copy-start
  7.2 135.1 %copy-start.2 = (bf16[768,768]{1,0:T(8,128)(2,1)S(1)}, bf16[768,768]{1,0:T(8,128)(2,1)}, u32[]{:S(2)}) copy-start(bf16[768,768]{1,0:T(8,128)(2,1)} %param.7) | copy-start | bytes 3538948
  7.2 135.1 %all-gather.3.cloned.1.call-start = ((), (), s32[]{:S(2)}) async-start(), calls=%async_computation.1 | async-start | bytes 6684672 | tf_op jit(solution)/shard_map/all_gather | solution.py:20
  101.9 260.6 %all-reduce.8.cloned.1.call-start = ((), (), s32[]{:S(2)}) async-start(), calls=%async_computation.2 | async-start | bytes 6291456 | tf_op jit(solution)/shard_map/psum | solution.py:26
  236.6 300.5 %all-reduce.14.cloned.1.call-start = ((), (), s32[]{:S(2)}) async-start(), calls=%async_computation.7 | async-start | bytes 3145728 | tf_op jit(solution)/shard_map/psum | solution.py:35
  241.3 295.8 %copy-start.4 = (f32[768]{0:T(1024)S(1)}, f32[768]{0:T(1024)}, u32[]{:S(2)}) copy-start(f32[768]{0:T(1024)} %param.9) | copy-start | bytes 9220
  368.0 304.3 %all-reduce.10.cloned.1.call-start = ((), (), s32[]{:S(2)}) async-start(), calls=%async_computation.3 | async-start | bytes 6291456 | tf_op jit(solution)/shard_map/psum | solution.py:26
  538.6 5.7 copy-start.1
  544.3 299.1 %copy-start.3 = (bf16[256,768]{1,0:T(8,128)(2,1)S(1)}, bf16[256,768]{1,0:T(8,128)(2,1)}, u32[]{:S(2)}) copy-start(bf16[256,768]{1,0:T(8,128)(2,1)} %all-reduce.15) | copy-start | bytes 1179652
  544.4 299.1 %all-reduce.12.cloned.1.call-start = ((), (), s32[]{:S(2)}) async-start(), calls=%async_computation.4 | async-start | bytes 1572864 | tf_op jit(solution)/shard_map/psum | solution.py:17
  678.0 210.4 %all-gather.5.cloned.1.call-start = ((), (), s32[]{:S(2)}) async-start(), calls=%async_computation.5 | async-start | bytes 6684672 | tf_op jit(solution)/shard_map/all_gather | solution.py:20
  845.4 252.9 %reduce-scatter.2.cloned.1.call-start = ((), (), s32[]{:S(2)}) async-start(), calls=%async_computation.6 | async-start | bytes 835584 | tf_op jit(solution)/shard_map/reduce_scatter | solution.py:48
Sparse Core Ops, SparseCore 0:
  102.0 40.2 all-gather.2
  236.8 125.6 all-reduce.7
  368.2 168.9 all-reduce.13
  544.5 127.8 all-reduce.9
  678.1 165.2 all-reduce.11
  845.5 42.8 all-gather.4
  892.8 205.5 reduce-scatter.1
where the time goes:
time: 1110 us
  waiting for transfers between devices  874 us (79%)
  blocking collectives  177 us (16%)
  matrix products  34.7 us (3%)
  between operations  14.2 us (1%)
    psum x2, waiting for transfers between devices, marker_terms(): total = lax.psum(partial_value, 'anim')  249 us
    reduce_scatter x1, waiting for transfers between devices, local(): lax.psum_scatter(out_partial, 'snp', scatter_dimension=1, tiled=True)  208 us
    psum x1, waiting for transfers between devices, local(): noncore_vals = lax.psum(noncore_partial, 'snp')  169 us
    psum x1, waiting for transfers between devices, core_columns(): summed = lax.psum(partial_value, 'snp')  165 us
    psum x1, blocking collectives, core_columns(): summed = lax.psum(partial_value, 'snp')  89.5 us
    psum x1, blocking collectives, local(): core_weights = lax.psum(weight_partial, 'snp').astype(jnp.bfloat16)  87.3 us
    all_gather x2, waiting for transfers between devices, core_columns(): whole = lax.all_gather(block, 'anim', axis=1, tiled=True)  83.3 us
    dot_general x6, matrix products, contract_last(): lax.dot_general(left, right, (((1,), (1,)), ((), ())), preferred_element_...  23.5 us
  transfers between devices with their start and end apart: 7, of which 7 were waited for; matrix products, arithmetic and copies ran while one was open for 0% of the time, Pallas kernels for 0%

commit v1 on v0

v1 whole, which is shorter than its diff:
```python
import functools

import jax
import jax.numpy as jnp
from jax import lax
from jax.experimental import pallas as pl
from jax.experimental.pallas import tpu as pltpu
from jax.sharding import PartitionSpec as P

NSNP = 49152
MESH = pl.DeviceIdType.MESH
BATCHES = 2
COL_SPLIT = 2
LAG = 3

f32 = jnp.float32
bf16 = jnp.bfloat16


def nt_dot(left, right):
    return lax.dot_general(
        left, right, (((1,), (1,)), ((), ())), preferred_element_type=f32
    )


def kernel(dims, core_hbm, noncore_hbm, inv_hbm, effects_hbm, scale_hbm,
           noncore_hbm_out, out_ref, *scratch):
    A, S, R, NA, NS, NI = dims
    NB, KC = BATCHES, COL_SPLIT
    Rb = R // NB
    KR = S // KC
    RC, W = Rb // KR, NA // KC
    chips = A // 2
    RA, H = Rb // chips, NS // 2
    OC = NA // S
    TN = min(256, NA)
    TE = min(512, H)
    (core, noncore, inv, effects, scale,
     pa, np_, ra, cv, tb, vc,
     pd, rd, wc, wf,
     xe, xr, ye, yb, re_, ze, me,
     pf, rf, nc, nf,
     xg, xh, yg, yc, rg, zg, mg,
     ph, rh, cr, tr, vr,
     op, ri,
     insem, outsem, send, recv, agsem) = scratch
    a = lax.axis_index("anim")
    s = lax.axis_index("snp")
    chip = a // 2
    half = a % 2
    partner = a + 1 - 2 * half

    loads = [(effects_hbm, effects), (core_hbm, core), (noncore_hbm, noncore),
             (inv_hbm, inv), (scale_hbm, scale)]
    copies = [pltpu.make_async_copy(x, y, insem.at[i]) for i, (x, y) in enumerate(loads)]
    for c in copies:
        c.start()

    barrier = pltpu.get_barrier_semaphore()

    def greet_snp(r, _):
        pl.semaphore_signal(barrier, inc=1, device_id={"snp": (s + r) % S}, device_id_type=MESH)
        return 0

    def greet_anim(r, _):
        pl.semaphore_signal(barrier, inc=1, device_id={"anim": (a + r) % A}, device_id_type=MESH)
        return 0

    lax.fori_loop(1, S, greet_snp, 0)
    lax.fori_loop(1, A, greet_anim, 0)

    @pl.when(a != s)
    def _():
        pl.semaphore_signal(barrier, inc=1, device_id={"anim": s, "snp": a}, device_id_type=MESH)
        pl.semaphore_wait(barrier, S + A - 1)

    @pl.when(a == s)
    def _():
        pl.semaphore_wait(barrier, S + A - 2)

    def rows(k):
        return pl.ds(pl.multiple_of((k % KR) * RC, RC), RC)

    def cols(k):
        return pl.ds(pl.multiple_of((k // KR) * W, W), W)

    def wait_bytes(ref, sem):
        pltpu.make_async_copy(ref, ref, sem).wait()

    ends = []

    def rs_snp(b, phase, part, got):
        def step(r, _):
            k = (s + r) % S
            pltpu.make_async_remote_copy(
                part.at[b, rows(k), cols(k)], got.at[b, r - 1],
                send.at[b, phase], recv.at[b, phase],
                device_id={"snp": k}, device_id_type=MESH).start()
            return 0
        lax.fori_loop(1, S, step, 0)
        ends.append((got.at[b], b, phase))

    def sum_snp(b, phase, part, got):
        wait_bytes(got.at[b], recv.at[b, phase])
        total = part[b, rows(s), cols(s)].astype(f32)
        for r in range(S - 1):
            total = total + got[b, r].astype(f32)
        return total

    def ag_snp(b, phase, chunk, whole, proxy):
        def step(r, _):
            pltpu.make_async_remote_copy(
                chunk.at[b], whole.at[b, rows(s), cols(s)],
                send.at[b, phase], recv.at[b, phase],
                device_id={"snp": (s + r) % S}, device_id_type=MESH).start()
            return 0
        lax.fori_loop(1, S, step, 0)
        whole[b, rows(s), cols(s)] = chunk[b]
        ends.append((proxy.at[b], b, phase))

    def turn(b, phase, chunk, landed):
        @pl.when(a != s)
        def _():
            pltpu.make_async_remote_copy(
                chunk.at[b], landed.at[b], send.at[b, phase], recv.at[b, phase],
                device_id={"anim": s, "snp": a}, device_id_type=MESH).start()

        @pl.when(a == s)
        def _():
            pltpu.make_async_copy(chunk.at[b], landed.at[b], recv.at[b, phase]).start()
        ends.append((None, b, phase))

    def ag_anim(b, turned, phase, landed, whole, proxy):
        wait_bytes(landed.at[b], recv.at[b, turned])

        def step(r, _):
            pltpu.make_async_remote_copy(
                landed.at[b], whole.at[b, rows(a), cols(a)],
                send.at[b, phase], recv.at[b, phase],
                device_id={"anim": (a + r) % A}, device_id_type=MESH).start()
            return 0
        lax.fori_loop(1, A, step, 0)
        whole[b, rows(a), cols(a)] = landed[b]
        ends.append((proxy.at[b], b, phase))

    def marker_product(b, phase, left, geno, out_half, in_half, own):
        lhs = left[b]

        def other(t, _):
            at = pl.ds(pl.multiple_of((1 - half) * H + t * TE, TE), TE)
            to = pl.ds(pl.multiple_of(t * TE, TE), TE)
            out_half[b, :, to] = jnp.dot(lhs, geno[:, at], preferred_element_type=f32).astype(bf16)
            pltpu.make_async_remote_copy(
                out_half.at[b, :, to], in_half.at[b, :, to],
                send.at[b, phase], recv.at[b, phase],
                device_id={"anim": partner}, device_id_type=MESH).start()
            return 0
        lax.fori_loop(0, H // TE, other, 0)

        def mine(t, _):
            at = pl.ds(pl.multiple_of(half * H + t * TE, TE), TE)
            to = pl.ds(pl.multiple_of(t * TE, TE), TE)
            own[b, :, to] = jnp.dot(lhs, geno[:, at], preferred_element_type=f32)
            return 0
        lax.fori_loop(0, H // TE, mine, 0)
        ends.append((in_half.at[b], b, phase))

    def chip_rows(c):
        return pl.ds(pl.multiple_of(c * RA, RA), RA)

    def rs_chips(b, crossed, phase, in_half, own, both, got):
        wait_bytes(in_half.at[b], recv.at[b, crossed])

        def step(r, _):
            c = (chip + r) % chips
            at = chip_rows(c)
            both[b, at, :] = (own[b, at, :] + in_half[b, at, :].astype(f32)).astype(bf16)
            pltpu.make_async_remote_copy(
                both.at[b, at, :], got.at[b, r - 1],
                send.at[b, phase], recv.at[b, phase],
                device_id={"anim": 2 * c + half}, device_id_type=MESH).start()
            return 0
        lax.fori_loop(1, chips, step, 0)
        ends.append((got.at[b], b, phase))

    def half_cols(h):
        return pl.ds(pl.multiple_of(h * H, H), H)

    def ag_chips(b, summed, phase, cross, slot, in_half, own, got, chunk, whole):
        at = chip_rows(chip)
        total = own[b, at, :] + in_half[b, at, :].astype(f32)
        wait_bytes(got.at[b], recv.at[b, summed])
        for r in range(chips - 1):
            total = total + got[b, r].astype(f32)
        chunk[b] = (total / NSNP).astype(bf16)
        spot = whole.at[b, at, half_cols(half)]

        def step(r, _):
            pltpu.make_async_remote_copy(
                chunk.at[b], spot, send.at[b, phase], agsem.at[b, slot, r - 1],
                device_id={"anim": 2 * ((chip + r) % chips) + half}, device_id_type=MESH).start()
            return 0
        lax.fori_loop(1, chips, step, 0)
        pltpu.make_async_remote_copy(
            chunk.at[b], spot, send.at[b, cross], recv.at[b, cross],
            device_id={"anim": partner}, device_id_type=MESH).start()
        whole[b, at, half_cols(half)] = chunk[b]
        ends.append((got.at[b], b, phase))
        ends.append((in_half.at[b], b, cross))

    def relay(b, cross, slot, whole):
        def step(r, _):
            c = (chip + chips - r) % chips
            spot = whole.at[b, chip_rows(c), half_cols(half)]
            wait_bytes(spot, agsem.at[b, slot, r - 1])
            pltpu.make_async_remote_copy(
                spot, spot, send.at[b, cross], recv.at[b, cross],
                device_id={"anim": partner}, device_id_type=MESH).start()
            return 0
        lax.fori_loop(1, chips, step, 0)

    def rep_rows(b):
        return pl.ds(b * Rb, Rb)

    def tiles(body):
        def step(t, _):
            body(pl.ds(pl.multiple_of(t * TN, TN), TN))
            return 0
        lax.fori_loop(0, NA // TN, step, 0)

    def s0(b):
        if b == 0:
            copies[0].wait()
            copies[1].wait()

        def body(at):
            pa[b, :, at] = nt_dot(effects[rep_rows(b), :], core[at, :]).astype(bf16)
        tiles(body)
        rs_snp(b, 0, pa, ra)

    def s0b(b):
        if b == 0:
            copies[2].wait()

        def body(at):
            np_[b, :, at] = nt_dot(effects[rep_rows(b), :], noncore[at, :])
        tiles(body)

    def s1(b):
        cv[b] = sum_snp(b, 0, pa, ra).astype(bf16)
        turn(b, 1, cv, tb)

    def s2(b):
        ag_anim(b, 1, 2, tb, vc, ra)

    def s3(b):
        if b == 0:
            copies[3].wait()
        wait_bytes(ra.at[b], recv.at[b, 2])

        def body(at):
            pd[b, :, at] = nt_dot(vc[b], inv[at, :]).astype(bf16)
        tiles(body)
        rs_snp(b, 3, pd, rd)

    def s4(b):
        wc[b] = sum_snp(b, 3, pd, rd).astype(bf16)
        ag_snp(b, 4, wc, wf, rd)

    def s5(b):
        wait_bytes(rd.at[b], recv.at[b, 4])
        marker_product(b, 5, wf, core, xe, xr, ye)

    def s6(b):
        rs_chips(b, 5, 6, xr, ye, yb, re_)

    def s7(b):
        ag_chips(b, 6, 7, 8, 0, xr, ye, re_, ze, me)

    def s8(b):
        relay(b, 8, 0, me)

    def s9(b):
        wait_bytes(xr.at[b], recv.at[b, 8])

        def body(at):
            pf[b, :, at] = (np_[b, :, at] - nt_dot(me[b], noncore[at, :])).astype(bf16)
        tiles(body)
        rs_snp(b, 9, pf, rf)

    def s10(b):
        if b == 0:
            copies[4].wait()
        nc[b] = (scale[:, cols(s)] * sum_snp(b, 9, pf, rf)).astype(bf16)
        ag_snp(b, 10, nc, nf, rf)

    def s11(b):
        wait_bytes(rf.at[b], recv.at[b, 10])
        pltpu.make_async_copy(nf.at[b], noncore_hbm_out.at[rep_rows(b), :], outsem.at[b]).start()
        marker_product(b, 11, nf, noncore, xg, xh, yg)

    def s12(b):
        rs_chips(b, 11, 12, xh, yg, yc, rg)

    def s13(b):
        ag_chips(b, 12, 13, 14, 1, xh, yg, rg, zg, mg)

    def s14(b):
        relay(b, 14, 1, mg)

    def s15(b):
        wait_bytes(xh.at[b], recv.at[b, 14])

        def body(at):
            ph[b, :, at] = nt_dot(mg[b], core[at, :]).astype(bf16)
        tiles(body)
        rs_snp(b, 15, ph, rh)

    def s16(b):
        cr[b] = (cv[b].astype(f32) - sum_snp(b, 15, ph, rh)).astype(bf16)
        turn(b, 16, cr, tr)

    def s17(b):
        ag_anim(b, 16, 17, tr, vr, rh)

    def s18(b):
        wait_bytes(rh.at[b], recv.at[b, 17])

        def body(at):
            op[b, at, :] = nt_dot(inv[at, :], vr[b]).astype(bf16)
        tiles(body)

        def step(r, _):
            k = (s + r) % S
            pltpu.make_async_remote_copy(
                op.at[b, pl.ds(pl.multiple_of(k * OC, OC), OC), :], ri.at[b, r - 1],
                send.at[b, 18], recv.at[b, 18],
                device_id={"snp": k}, device_id_type=MESH).start()
            return 0
        lax.fori_loop(1, S, step, 0)
        ends.append((ri.at[b], b, 18))

    def s19(b):
        wait_bytes(ri.at[b], recv.at[b, 18])
        total = op[b, pl.ds(pl.multiple_of(s * OC, OC), OC), :].astype(f32)
        for r in range(S - 1):
            total = total + ri[b, r].astype(f32)
        out_ref[:, b * Rb:(b + 1) * Rb] = total

    stages = [s0, s0b, s1, s2, s3, s4, s5, s6, s7, s8, s9, s10, s11, s12, s13,
              s14, s15, s16, s17, s18, s19]
    order = sorted((i + LAG * b, b, i) for i in range(len(stages)) for b in range(NB))
    for _, b, i in order:
        stages[i](b)

    for ref, b, phase in ends:
        if ref is None:
            @pl.when(a != s)
            def _():
                wait_bytes(tb.at[b], send.at[b, phase])
        else:
            wait_bytes(ref, send.at[b, phase])
    for b in range(NB):
        wait_bytes(nf.at[b], outsem.at[b])


def solution(mesh):
    A, S = mesh.shape["anim"], mesh.shape["snp"]

    def local(core_geno, noncore_geno, core_inv, snp_effects, noncore_scale):
        R = snp_effects.shape[0]
        NA, NS = core_geno.shape
        NI = core_inv.shape[1]
        NB, KC = BATCHES, COL_SPLIT
        Rb = R // NB
        KR = S // KC
        RC, W = Rb // KR, NA // KC
        chips = A // 2
        RA, H = Rb // chips, NS // 2
        OC = NA // S
        V = pltpu.VMEM
        chunk = V((NB, RC, W), bf16)
        part = V((NB, Rb, NA), bf16)
        got = V((NB, S - 1, RC, W), bf16)
        halfb = V((NB, Rb, H), bf16)
        marker = [halfb, halfb, V((NB, Rb, H), f32), halfb,
                  V((NB, chips - 1, RA, H), bf16), V((NB, RA, H), bf16), V((NB, Rb, NS), bf16)]
        scratch = [
            V((NA, NS), bf16), V((NA, NS), bf16), V((NA, NI), bf16), V((R, NS), bf16), V((1, NA), f32),
            part, V((NB, Rb, NA), f32), got, chunk, chunk, part,
            part, got, chunk, part,
            *marker,
            part, got, chunk, part,
            *marker,
            part, got, chunk, chunk, part,
            V((NB, NA, Rb), bf16), V((NB, S - 1, OC, Rb), bf16),
            pltpu.SemaphoreType.DMA((5,)), pltpu.SemaphoreType.DMA((NB,)),
            pltpu.SemaphoreType.DMA((NB, 19)), pltpu.SemaphoreType.DMA((NB, 19)),
            pltpu.SemaphoreType.DMA((NB, 2, chips - 1)),
        ]
        half_out, turned = pl.pallas_call(
            functools.partial(kernel, (A, S, R, NA, NS, NI)),
            out_shape=(jax.ShapeDtypeStruct((R, NA), bf16), jax.ShapeDtypeStruct((OC, R), f32)),
            in_specs=[pl.BlockSpec(memory_space=pl.ANY)] * 5,
            out_specs=(pl.BlockSpec(memory_space=pl.ANY), pl.BlockSpec(memory_space=pltpu.VMEM)),
            scratch_shapes=scratch,
            compiler_params=pltpu.CompilerParams(
                collective_id=0, has_side_effects=True, vmem_limit_bytes=60 * 1024 * 1024),
        )(core_geno, noncore_geno, core_inv, snp_effects, noncore_scale.reshape(1, -1))
        return half_out.astype(f32), turned.T

    return jax.shard_map(
        local,
        mesh=mesh,
        in_specs=(P("anim", "snp"), P("anim", "snp"), P("anim", "snp"), P(None, "snp"), P("anim")),
        out_specs=(P(None, "anim"), P(None, ("anim", "snp"))),
        check_vma=False,
    )
```

time: 1110 us -> 182 us (0.16)
  waiting for transfers between devices: 874 us -> 0 us
  blocking collectives: 177 us -> 0 us
  Pallas kernels: 0 us -> 174 us
  matrix products: 34.7 us -> 0 us
  between operations: 14.2 us -> 0.64 us
    psum x4 -> x0, waiting for transfers between devices: 583 us -> none  [the longest x2 249 us: marker_terms(): total = lax.psum(partial_value, 'anim')]
    reduce_scatter x1 -> x0, waiting for transfers between devices: 208 us -> none  [local(): lax.psum_scatter(out_partial, 'snp', scatter_dimension=1, tiled=True)]
    psum x2 -> x0, blocking collectives: 177 us -> none  [the longest x1 89.5 us: core_columns(): summed = lax.psum(partial_value, 'snp')]
    pallas_call x0 -> x1, Pallas kernels: none -> 174 us  [local(): pl.pallas_call(functools.partial(kernel, (A, S, R, NA, NS, NI)), out_shap...]
    all_gather x2 -> x0, waiting for transfers between devices: 83.3 us -> none  [core_columns(): whole = lax.all_gather(block, 'anim', axis=1, tiled=True)]
    dot_general x8 -> x0, matrix products: 34.7 us -> none  [the longest x6 23.5 us: contract_last(): lax.dot_general(left, right, (((1,), (1,)), ((), ())), preferred_element_...]
  transfers between devices with their start and end apart: 7 -> 0, of which waited for: 7 -> 0; matrix products, arithmetic and copies ran while one was open for 0% -> 0% of each run, Pallas kernels for 0% -> 0%
where the time goes in v1:
time: 182 us; the launch traced here: 180 us
  Pallas kernels  174 us (96%)
  local copies, waits for them, and re-layouts  2.69 us (1%)
  other arithmetic  1.93 us (1%)
    pallas_call x1, Pallas kernels, local(): pl.pallas_call(functools.partial(kernel, (A, S, R, NA, NS, NI)), out_shap...  174 us

profile of v1, /device:TPU:8, one launch (start us, length us, event | category | flops | bytes accessed | tf_op | source)
XLA Modules:
  0.0 179.5 jit_solution(9180478706557434758)
XLA Ops:
  0.6 1.3 reshape.7.scale_hbm
  1.9 174.3 %shard_map.68 = (bf16[256,768]{1,0:T(8,128)(2,1)}, f32[48,256]{1,0:T(8,128)}) custom-call(bf16[768,3072]{1,0:T(8,128)(2,1)} %core_hbm.1, bf16[768,3072]{1,0:T(8,128)(2,1)} %noncore_hbm.1, bf16[768,768]{1,0:T(8,128)(2,1)} %inv_hbm.1, bf16[256,3072]{1,0:T(8,128)(2,1)} %effects_hbm.1, f32[1,768]{1,0:T(1,128)} %reshape.7.scale_hbm), custom_call_target="tpu_custom_call" | custom-call | tf_op jit(solution)/shard_map/pallas_call | solution.py:401
  176.2 1.9 %convert_element_type.3 = f32[256,768]{1,0:T(8,128)} convert(bf16[256,768]{1,0:T(8,128)(2,1)} %get-tuple-element.4) | non-fusion elementwise | flops 196608 | bytes 1179648 | tf_op jit(solution)/shard_map/convert_element_type | solution.py:410
  178.1 1.4 copy.8

commit v2 on v1

--- a/solution.py
+++ b/solution.py
@@ -11,7 +11,7 @@
 MESH = pl.DeviceIdType.MESH
 BATCHES = 2
 COL_SPLIT = 2
-LAG = 3
+LAG = 1
 
 f32 = jnp.float32
 bf16 = jnp.bfloat16
@@ -33,7 +33,7 @@
     chips = A // 2
     RA, H = Rb // chips, NS // 2
     OC = NA // S
-    TN = min(256, NA)
+    TN = min(256, W)
     TE = min(512, H)
     (core, noncore, inv, effects, scale,
      pa, np_, ra, cv, tb, vc,
@@ -50,6 +50,15 @@
     half = a % 2
     partner = a + 1 - 2 * half
 
+    fold = S // 4
+    away = (s // 2 + S // 2 - a // 2) % (S // 2)
+    near = away // fold
+    drop = near * (away - fold) + (1 - near) * (fold - 1 - away)
+    turn_row = (((a // 4 + drop) % (A // 4)) * 2 + ((a // 2) % 2 + s % 2 + a % 2) % 2) * 2 + 1 - near
+    rise = (a // 4 + A // 4 - s // 4) % (A // 4)
+    reach = half * (fold - 1 - rise) + (1 - half) * (fold + rise)
+    index = ((s // 2 + reach) % (S // 2)) * 2 + (s % 2 + (a // 2) % 2 + (s // 2) % 2) % 2
+
     loads = [(effects_hbm, effects), (core_hbm, core), (noncore_hbm, noncore),
              (inv_hbm, inv), (scale_hbm, scale)]
     copies = [pltpu.make_async_copy(x, y, insem.at[i]) for i, (x, y) in enumerate(loads)]
@@ -69,35 +78,61 @@
     lax.fori_loop(1, S, greet_snp, 0)
     lax.fori_loop(1, A, greet_anim, 0)
 
-    @pl.when(a != s)
-    def _():
-        pl.semaphore_signal(barrier, inc=1, device_id={"anim": s, "snp": a}, device_id_type=MESH)
+    pl.semaphore_signal(barrier, inc=1, device_id={"anim": s, "snp": index}, device_id_type=MESH)
+
+    def meet():
         pl.semaphore_wait(barrier, S + A - 1)
 
-    @pl.when(a == s)
-    def _():
-        pl.semaphore_wait(barrier, S + A - 2)
+    def ring_step(j, n):
+        return ((n - j) // 2) * (2 * (j % 2) - 1) % n
+
+    rings, circles = S // 2, chips // 2
+    snp_z, snp_x = s // 2, s % 2
+    anim_y, anim_x = chip // 2, chip % 2
+    flip = 1 - snp_x, snp_x
+    side = 1 - anim_x, anim_x
+    snp_peers = [lax.rem(snp_z + ring_step(i // 2, rings), rings) * 2 + flip[i % 2] for i in range(S - 1)]
+    chip_peers = [lax.rem(anim_y + ring_step(i // 2, circles), circles) * 2 + side[i % 2] for i in range(chips - 1)]
+    chip_backs = [lax.rem(anim_y + circles - ring_step(i // 2, circles), circles) * 2 + side[i % 2] for i in range(chips - 1)]
+    anim_peers = [
+        (lax.rem(anim_y + ring_step(i // 4, circles), circles) * 2 + side[i % 4 // 2]) * 2
+        + (1 - half if i % 2 == 0 else half) for i in range(A - 1)]
 
     def rows(k):
-        return pl.ds(pl.multiple_of((k % KR) * RC, RC), RC)
+        return pl.ds(pl.multiple_of((k // KC) * RC, RC), RC)
 
     def cols(k):
-        return pl.ds(pl.multiple_of((k // KR) * W, W), W)
+        return pl.ds(pl.multiple_of((k % KC) * W, W), W)
 
     def wait_bytes(ref, sem):
         pltpu.make_async_copy(ref, ref, sem).wait()
 
     ends = []
 
-    def rs_snp(b, phase, part, got):
-        def step(r, _):
-            k = (s + r) % S
-            pltpu.make_async_remote_copy(
-                part.at[b, rows(k), cols(k)], got.at[b, r - 1],
+    def send_part(b, phase, part, got, which):
+        for r in which:
+            k = snp_peers[r]
+            pltpu.make_async_remote_copy(
+                part.at[b, rows(k), cols(k)], got.at[b, r],
                 send.at[b, phase], recv.at[b, phase],
                 device_id={"snp": k}, device_id_type=MESH).start()
+
+    def rs_snp(b, phase, part, got):
+        send_part(b, phase, part, got, range(S - 1))
+        ends.append((got.at[b], b, phase))
+
+    def tiles_rs_snp(b, phase, part, got, body):
+        count = NA // TN
+        early = -(-W // TN)
+
+        def step(t, _):
+            at = snp_x * t + (1 - snp_x) * (count - 1 - t)
+            body(pl.ds(pl.multiple_of(at * TN, TN), TN))
             return 0
-        lax.fori_loop(1, S, step, 0)
+        lax.fori_loop(0, early, step, 0)
+        send_part(b, phase, part, got, range(0, S - 1, 2))
+        lax.fori_loop(early, count, step, 0)
+        send_part(b, phase, part, got, range(1, S - 1, 2))
         ends.append((got.at[b], b, phase))
 
     def sum_snp(b, phase, part, got):
@@ -108,39 +143,29 @@
         return total
 
     def ag_snp(b, phase, chunk, whole, proxy):
-        def step(r, _):
+        for r in range(S - 1):
             pltpu.make_async_remote_copy(
                 chunk.at[b], whole.at[b, rows(s), cols(s)],
                 send.at[b, phase], recv.at[b, phase],
-                device_id={"snp": (s + r) % S}, device_id_type=MESH).start()
-            return 0
-        lax.fori_loop(1, S, step, 0)
+                device_id={"snp": snp_peers[r]}, device_id_type=MESH).start()
         whole[b, rows(s), cols(s)] = chunk[b]
         ends.append((proxy.at[b], b, phase))
 
     def turn(b, phase, chunk, landed):
-        @pl.when(a != s)
-        def _():
-            pltpu.make_async_remote_copy(
-                chunk.at[b], landed.at[b], send.at[b, phase], recv.at[b, phase],
-                device_id={"anim": s, "snp": a}, device_id_type=MESH).start()
-
-        @pl.when(a == s)
-        def _():
-            pltpu.make_async_copy(chunk.at[b], landed.at[b], recv.at[b, phase]).start()
-        ends.append((None, b, phase))
+        pltpu.make_async_remote_copy(
+            chunk.at[b], landed.at[b], send.at[b, phase], recv.at[b, phase],
+            device_id={"anim": turn_row, "snp": a}, device_id_type=MESH).start()
+        ends.append((landed.at[b], b, phase))
 
     def ag_anim(b, turned, phase, landed, whole, proxy):
         wait_bytes(landed.at[b], recv.at[b, turned])
 
-        def step(r, _):
-            pltpu.make_async_remote_copy(
-                landed.at[b], whole.at[b, rows(a), cols(a)],
+        for r in range(A - 1):
+            pltpu.make_async_remote_copy(
+                landed.at[b], whole.at[b, rows(index), cols(index)],
                 send.at[b, phase], recv.at[b, phase],
-                device_id={"anim": (a + r) % A}, device_id_type=MESH).start()
-            return 0
-        lax.fori_loop(1, A, step, 0)
-        whole[b, rows(a), cols(a)] = landed[b]
+                device_id={"anim": anim_peers[r]}, device_id_type=MESH).start()
+        whole[b, rows(index), cols(index)] = landed[b]
         ends.append((proxy.at[b], b, phase))
 
     def marker_product(b, phase, left, geno, out_half, in_half, own):
@@ -171,16 +196,14 @@
     def rs_chips(b, crossed, phase, in_half, own, both, got):
         wait_bytes(in_half.at[b], recv.at[b, crossed])
 
-        def step(r, _):
-            c = (chip + r) % chips
+        for r in range(chips - 1):
+            c = chip_peers[r]
             at = chip_rows(c)
             both[b, at, :] = (own[b, at, :] + in_half[b, at, :].astype(f32)).astype(bf16)
             pltpu.make_async_remote_copy(
-                both.at[b, at, :], got.at[b, r - 1],
+                both.at[b, at, :], got.at[b, r],
                 send.at[b, phase], recv.at[b, phase],
                 device_id={"anim": 2 * c + half}, device_id_type=MESH).start()
-            return 0
-        lax.fori_loop(1, chips, step, 0)
         ends.append((got.at[b], b, phase))
 
     def half_cols(h):
@@ -195,12 +218,10 @@
         chunk[b] = (total / NSNP).astype(bf16)
         spot = whole.at[b, at, half_cols(half)]
 
-        def step(r, _):
-            pltpu.make_async_remote_copy(
-                chunk.at[b], spot, send.at[b, phase], agsem.at[b, slot, r - 1],
-                device_id={"anim": 2 * ((chip + r) % chips) + half}, device_id_type=MESH).start()
-            return 0
-        lax.fori_loop(1, chips, step, 0)
+        for r in range(chips - 1):
+            pltpu.make_async_remote_copy(
+                chunk.at[b], spot, send.at[b, phase], agsem.at[b, slot, r],
+                device_id={"anim": 2 * chip_peers[r] + half}, device_id_type=MESH).start()
         pltpu.make_async_remote_copy(
             chunk.at[b], spot, send.at[b, cross], recv.at[b, cross],
             device_id={"anim": partner}, device_id_type=MESH).start()
@@ -209,15 +230,12 @@
         ends.append((in_half.at[b], b, cross))
 
     def relay(b, cross, slot, whole):
-        def step(r, _):
-            c = (chip + chips - r) % chips
-            spot = whole.at[b, chip_rows(c), half_cols(half)]
-            wait_bytes(spot, agsem.at[b, slot, r - 1])
+        for r in range(chips - 1):
+            spot = whole.at[b, chip_rows(chip_backs[r]), half_cols(half)]
+            wait_bytes(spot, agsem.at[b, slot, r])
             pltpu.make_async_remote_copy(
                 spot, spot, send.at[b, cross], recv.at[b, cross],
                 device_id={"anim": partner}, device_id_type=MESH).start()
-            return 0
-        lax.fori_loop(1, chips, step, 0)
 
     def rep_rows(b):
         return pl.ds(b * Rb, Rb)
@@ -236,6 +254,10 @@
         def body(at):
             pa[b, :, at] = nt_dot(effects[rep_rows(b), :], core[at, :]).astype(bf16)
         tiles(body)
+
+    def s0a(b):
+        if b == 0:
+            meet()
         rs_snp(b, 0, pa, ra)
 
     def s0b(b):
@@ -260,8 +282,7 @@
 
         def body(at):
             pd[b, :, at] = nt_dot(vc[b], inv[at, :]).astype(bf16)
-        tiles(body)
-        rs_snp(b, 3, pd, rd)
+        tiles_rs_snp(b, 3, pd, rd, body)
 
     def s4(b):
         wc[b] = sum_snp(b, 3, pd, rd).astype(bf16)
@@ -280,18 +301,24 @@
     def s8(b):
         relay(b, 8, 0, me)
 
+        def body(at):
+            np_[b, :, at] = np_[b, :, at] - nt_dot(me[b, :, half_cols(half)], noncore[at, half_cols(half)])
+        tiles(body)
+
     def s9(b):
         wait_bytes(xr.at[b], recv.at[b, 8])
 
         def body(at):
-            pf[b, :, at] = (np_[b, :, at] - nt_dot(me[b], noncore[at, :])).astype(bf16)
-        tiles(body)
-        rs_snp(b, 9, pf, rf)
+            pf[b, :, at] = (np_[b, :, at] - nt_dot(
+                me[b, :, half_cols(1 - half)], noncore[at, half_cols(1 - half)])).astype(bf16)
+        tiles_rs_snp(b, 9, pf, rf, body)
 
     def s10(b):
         if b == 0:
             copies[4].wait()
-        nc[b] = (scale[:, cols(s)] * sum_snp(b, 9, pf, rf)).astype(bf16)
+        first = (s % KC) * (W // 128)
+        line = jnp.concatenate([scale[pl.ds(first + q, 1), :] for q in range(W // 128)], axis=1)
+        nc[b] = (line * sum_snp(b, 9, pf, rf)).astype(bf16)
         ag_snp(b, 10, nc, nf, rf)
 
     def s11(b):
@@ -308,13 +335,17 @@
     def s14(b):
         relay(b, 14, 1, mg)
 
+        def body(at):
+            np_[b, :, at] = nt_dot(mg[b, :, half_cols(half)], core[at, half_cols(half)])
+        tiles(body)
+
     def s15(b):
         wait_bytes(xh.at[b], recv.at[b, 14])
 
         def body(at):
-            ph[b, :, at] = nt_dot(mg[b], core[at, :]).astype(bf16)
-        tiles(body)
-        rs_snp(b, 15, ph, rh)
+            ph[b, :, at] = (np_[b, :, at] + nt_dot(
+                mg[b, :, half_cols(1 - half)], core[at, half_cols(1 - half)])).astype(bf16)
+        tiles_rs_snp(b, 15, ph, rh, body)
 
     def s16(b):
         cr[b] = (cv[b].astype(f32) - sum_snp(b, 15, ph, rh)).astype(bf16)
@@ -326,18 +357,14 @@
     def s18(b):
         wait_bytes(rh.at[b], recv.at[b, 17])
 
-        def body(at):
-            op[b, at, :] = nt_dot(inv[at, :], vr[b]).astype(bf16)
-        tiles(body)
-
-        def step(r, _):
-            k = (s + r) % S
-            pltpu.make_async_remote_copy(
-                op.at[b, pl.ds(pl.multiple_of(k * OC, OC), OC), :], ri.at[b, r - 1],
+        op[b] = nt_dot(inv[...], vr[b]).astype(bf16)
+
+        for r in range(S - 1):
+            k = snp_peers[r]
+            pltpu.make_async_remote_copy(
+                op.at[b, pl.ds(pl.multiple_of(k * OC, OC), OC), :], ri.at[b, r],
                 send.at[b, 18], recv.at[b, 18],
                 device_id={"snp": k}, device_id_type=MESH).start()
-            return 0
-        lax.fori_loop(1, S, step, 0)
         ends.append((ri.at[b], b, 18))
 
     def s19(b):
@@ -347,21 +374,21 @@
             total = total + ri[b, r].astype(f32)
         out_ref[:, b * Rb:(b + 1) * Rb] = total
 
-    stages = [s0, s0b, s1, s2, s3, s4, s5, s6, s7, s8, s9, s10, s11, s12, s13,
+    stages = [s0, s0a, s0b, s1, s2, s3, s4, s5, s6, s7, s8, s9, s10, s11, s12, s13,
               s14, s15, s16, s17, s18, s19]
     order = sorted((i + LAG * b, b, i) for i in range(len(stages)) for b in range(NB))
     for _, b, i in order:
         stages[i](b)
 
     for ref, b, phase in ends:
-        if ref is None:
-            @pl.when(a != s)
-            def _():
-                wait_bytes(tb.at[b], send.at[b, phase])
-        else:
-            wait_bytes(ref, send.at[b, phase])
+        wait_bytes(ref, send.at[b, phase])
     for b in range(NB):
         wait_bytes(nf.at[b], outsem.at[b])
+
+
+def widen(half_ref, turned_ref, noncore_ref, core_ref):
+    noncore_ref[...] = half_ref[...].astype(f32)
+    core_ref[...] = turned_ref[...]
 
 
 def solution(mesh):
@@ -386,7 +413,7 @@
         marker = [halfb, halfb, V((NB, Rb, H), f32), halfb,
                   V((NB, chips - 1, RA, H), bf16), V((NB, RA, H), bf16), V((NB, Rb, NS), bf16)]
         scratch = [
-            V((NA, NS), bf16), V((NA, NS), bf16), V((NA, NI), bf16), V((R, NS), bf16), V((1, NA), f32),
+            V((NA, NS), bf16), V((NA, NS), bf16), V((NA, NI), bf16), V((R, NS), bf16), V((NA // 128, 128), f32),
             part, V((NB, Rb, NA), f32), got, chunk, chunk, part,
             part, got, chunk, part,
             *marker,
@@ -406,8 +433,12 @@
             scratch_shapes=scratch,
             compiler_params=pltpu.CompilerParams(
                 collective_id=0, has_side_effects=True, vmem_limit_bytes=60 * 1024 * 1024),
-        )(core_geno, noncore_geno, core_inv, snp_effects, noncore_scale.reshape(1, -1))
-        return half_out.astype(f32), turned.T
+        )(core_geno, noncore_geno, core_inv, snp_effects, noncore_scale.reshape(-1, 128))
+        noncore_out, core_out = pl.pallas_call(
+            widen,
+            out_shape=(jax.ShapeDtypeStruct((R, NA), f32), jax.ShapeDtypeStruct((OC, R), f32)),
+        )(half_out, turned)
+        return noncore_out, core_out.T
 
     return jax.shard_map(
         local,

time: 182 us -> 142 us (0.78)
  Pallas kernels: 174 us -> 140 us
  local copies, waits for them, and re-layouts: 2.69 us -> 0 us
  other arithmetic: 1.93 us -> 0 us
    pallas_call x1, Pallas kernels: 174 us -> 138 us  [local(): pl.pallas_call(functools.partial(kernel, (A, S, R, NA, NS, NI)), out_shap...]
    pallas_call x0 -> x1, Pallas kernels: none -> 1.94 us  [local(): pl.pallas_call(widen, out_shape=(jax.ShapeDtypeStruct((R, NA), f32), jax....]
    convert_element_type x1 -> x0, other arithmetic: 1.93 us -> none  [local(): return (half_out.astype(f32), turned.T)]
where the time goes in v2:
time: 142 us; the launch traced here: 141 us
  Pallas kernels  140 us (99%)
    pallas_call x1, Pallas kernels, local(): pl.pallas_call(functools.partial(kernel, (A, S, R, NA, NS, NI)), out_shap...  138 us

profile of v2, /device:TPU:8, one launch (start us, length us, event | category | flops | bytes accessed | tf_op | source)
XLA Modules:
  0.0 140.6 jit_solution(13894755872649503713)
XLA Ops:
  0.6 138.0 %shard_map.68 = (bf16[256,768]{1,0:T(8,128)(2,1)}, f32[48,256]{1,0:T(8,128)}) custom-call(bf16[768,3072]{1,0:T(8,128)(2,1)} %core_hbm.1, bf16[768,3072]{1,0:T(8,128)(2,1)} %noncore_hbm.1, bf16[768,768]{1,0:T(8,128)(2,1)} %inv_hbm.1, bf16[256,3072]{1,0:T(8,128)(2,1)} %effects_hbm.1, f32[6,128]{1,0:T(8,128)} %bitcast.2), custom_call_target="tpu_custom_call" | custom-call | tf_op jit(solution)/shard_map/pallas_call | solution.py:428
  138.7 1.9 %shard_map.69 = (f32[256,768]{1,0:T(8,128)}, f32[48,256]{1,0:T(8,128)}) custom-call(bf16[256,768]{1,0:T(8,128)(2,1)} %get-tuple-element.6.half_ref, f32[48,256]{1,0:T(8,128)} %get-tuple-element.7.turned_ref), custom_call_target="tpu_custom_call" | custom-call | tf_op jit(solution)/shard_map/pallas_call | solution.py:437

commit v3 on v2

--- a/solution.py
+++ b/solution.py
@@ -34,7 +34,7 @@
     RA, H = Rb // chips, NS // 2
     OC = NA // S
     TN = min(256, W)
-    TE = min(512, H)
+    TE = min(768, H)
     (core, noncore, inv, effects, scale,
      pa, np_, ra, cv, tb, vc,
      pd, rd, wc, wf,
@@ -59,27 +59,6 @@
     reach = half * (fold - 1 - rise) + (1 - half) * (fold + rise)
     index = ((s // 2 + reach) % (S // 2)) * 2 + (s % 2 + (a // 2) % 2 + (s // 2) % 2) % 2
 
-    loads = [(effects_hbm, effects), (core_hbm, core), (noncore_hbm, noncore),
-             (inv_hbm, inv), (scale_hbm, scale)]
-    copies = [pltpu.make_async_copy(x, y, insem.at[i]) for i, (x, y) in enumerate(loads)]
-    for c in copies:
-        c.start()
-
-    barrier = pltpu.get_barrier_semaphore()
-
-    def greet_snp(r, _):
-        pl.semaphore_signal(barrier, inc=1, device_id={"snp": (s + r) % S}, device_id_type=MESH)
-        return 0
-
-    def greet_anim(r, _):
-        pl.semaphore_signal(barrier, inc=1, device_id={"anim": (a + r) % A}, device_id_type=MESH)
-        return 0
-
-    lax.fori_loop(1, S, greet_snp, 0)
-    lax.fori_loop(1, A, greet_anim, 0)
-
-    pl.semaphore_signal(barrier, inc=1, device_id={"anim": s, "snp": index}, device_id_type=MESH)
-
     def meet():
         pl.semaphore_wait(barrier, S + A - 1)
 
@@ -98,6 +77,19 @@
         (lax.rem(anim_y + ring_step(i // 4, circles), circles) * 2 + side[i % 4 // 2]) * 2
         + (1 - half if i % 2 == 0 else half) for i in range(A - 1)]
 
+    barrier = pltpu.get_barrier_semaphore()
+    for k in snp_peers:
+        pl.semaphore_signal(barrier, inc=1, device_id={"snp": k}, device_id_type=MESH)
+    for k in anim_peers:
+        pl.semaphore_signal(barrier, inc=1, device_id={"anim": k}, device_id_type=MESH)
+    pl.semaphore_signal(barrier, inc=1, device_id={"anim": s, "snp": index}, device_id_type=MESH)
+
+    loads = [(effects_hbm, effects), (core_hbm, core), (noncore_hbm, noncore),
+             (inv_hbm, inv), (scale_hbm, scale)]
+    copies = [pltpu.make_async_copy(x, y, insem.at[i]) for i, (x, y) in enumerate(loads)]
+    for c in copies:
+        c.start()
+
     def rows(k):
         return pl.ds(pl.multiple_of((k // KC) * RC, RC), RC)
 
@@ -122,16 +114,11 @@
         ends.append((got.at[b], b, phase))
 
     def tiles_rs_snp(b, phase, part, got, body):
-        count = NA // TN
-        early = -(-W // TN)
-
-        def step(t, _):
-            at = snp_x * t + (1 - snp_x) * (count - 1 - t)
-            body(pl.ds(pl.multiple_of(at * TN, TN), TN))
-            return 0
-        lax.fori_loop(0, early, step, 0)
+        early = -(-W // TN) * TN
+        late = NA - early
+        body(pl.ds(pl.multiple_of((1 - snp_x) * late, TN), early))
         send_part(b, phase, part, got, range(0, S - 1, 2))
-        lax.fori_loop(early, count, step, 0)
+        body(pl.ds(pl.multiple_of(snp_x * early, TN), late))
         send_part(b, phase, part, got, range(1, S - 1, 2))
         ends.append((got.at[b], b, phase))
 
@@ -182,12 +169,7 @@
             return 0
         lax.fori_loop(0, H // TE, other, 0)
 
-        def mine(t, _):
-            at = pl.ds(pl.multiple_of(half * H + t * TE, TE), TE)
-            to = pl.ds(pl.multiple_of(t * TE, TE), TE)
-            own[b, :, to] = jnp.dot(lhs, geno[:, at], preferred_element_type=f32)
-            return 0
-        lax.fori_loop(0, H // TE, mine, 0)
+        own[b] = jnp.dot(lhs, geno[:, half_cols(half)], preferred_element_type=f32)
         ends.append((in_half.at[b], b, phase))
 
     def chip_rows(c):
@@ -240,11 +222,7 @@
     def rep_rows(b):
         return pl.ds(b * Rb, Rb)
 
-    def tiles(body):
-        def step(t, _):
-            body(pl.ds(pl.multiple_of(t * TN, TN), TN))
-            return 0
-        lax.fori_loop(0, NA // TN, step, 0)
+    everywhere = pl.ds(0, NA)
 
     def s0(b):
         if b == 0:
@@ -253,7 +231,7 @@
 
         def body(at):
             pa[b, :, at] = nt_dot(effects[rep_rows(b), :], core[at, :]).astype(bf16)
-        tiles(body)
+        body(everywhere)
 
     def s0a(b):
         if b == 0:
@@ -266,7 +244,7 @@
 
         def body(at):
             np_[b, :, at] = nt_dot(effects[rep_rows(b), :], noncore[at, :])
-        tiles(body)
+        body(everywhere)
 
     def s1(b):
         cv[b] = sum_snp(b, 0, pa, ra).astype(bf16)
@@ -303,7 +281,7 @@
 
         def body(at):
             np_[b, :, at] = np_[b, :, at] - nt_dot(me[b, :, half_cols(half)], noncore[at, half_cols(half)])
-        tiles(body)
+        body(everywhere)
 
     def s9(b):
         wait_bytes(xr.at[b], recv.at[b, 8])
@@ -337,7 +315,7 @@
 
         def body(at):
             np_[b, :, at] = nt_dot(mg[b, :, half_cols(half)], core[at, half_cols(half)])
-        tiles(body)
+        body(everywhere)
 
     def s15(b):
         wait_bytes(xh.at[b], recv.at[b, 14])
@@ -377,6 +355,7 @@
     stages = [s0, s0a, s0b, s1, s2, s3, s4, s5, s6, s7, s8, s9, s10, s11, s12, s13,
               s14, s15, s16, s17, s18, s19]
     order = sorted((i + LAG * b, b, i) for i in range(len(stages)) for b in range(NB))
+    order[-3], order[-2] = order[-2], order[-3]
     for _, b, i in order:
         stages[i](b)
 
@@ -436,7 +415,10 @@
         )(core_geno, noncore_geno, core_inv, snp_effects, noncore_scale.reshape(-1, 128))
         noncore_out, core_out = pl.pallas_call(
             widen,
+            grid=(2,),
             out_shape=(jax.ShapeDtypeStruct((R, NA), f32), jax.ShapeDtypeStruct((OC, R), f32)),
+            in_specs=[pl.BlockSpec((R // 2, NA), lambda g: (g, 0)), pl.BlockSpec((OC, R // 2), lambda g: (0, g))],
+            out_specs=(pl.BlockSpec((R // 2, NA), lambda g: (g, 0)), pl.BlockSpec((OC, R // 2), lambda g: (0, g))),
         )(half_out, turned)
         return noncore_out, core_out.T
 

time: 142 us -> 142 us (level)
  no operation moved by 1% of the time
where the time goes in v3:
time: 142 us; the launch traced here: 141 us
  Pallas kernels  140 us (99%)
    pallas_call x1, Pallas kernels, local(): pl.pallas_call(functools.partial(kernel, (A, S, R, NA, NS, NI)), out_shap...  138 us

profile of v3, /device:TPU:8, one launch (start us, length us, event | category | flops | bytes accessed | tf_op | source)
XLA Modules:
  0.0 140.6 jit_solution(136916964938263015)
XLA Ops:
  0.6 138.1 %shard_map.68 = (bf16[256,768]{1,0:T(8,128)(2,1)}, f32[48,256]{1,0:T(8,128)}) custom-call(bf16[768,3072]{1,0:T(8,128)(2,1)} %core_hbm.1, bf16[768,3072]{1,0:T(8,128)(2,1)} %noncore_hbm.1, bf16[768,768]{1,0:T(8,128)(2,1)} %inv_hbm.1, bf16[256,3072]{1,0:T(8,128)(2,1)} %effects_hbm.1, f32[6,128]{1,0:T(8,128)} %bitcast.2), custom_call_target="tpu_custom_call" | custom-call | tf_op jit(solution)/shard_map/pallas_call | solution.py:407
  138.8 1.9 %shard_map.69 = (f32[256,768]{1,0:T(8,128)}, f32[48,256]{1,0:T(8,128)}) custom-call(bf16[256,768]{1,0:T(8,128)(2,1)} %get-tuple-element.6.half_ref, f32[48,256]{1,0:T(8,128)} %get-tuple-element.7.turned_ref), custom_call_target="tpu_custom_call" | custom-call | tf_op jit(solution)/shard_map/pallas_call | solution.py:416
